TPU v7x, 256 devices: a whole 4x4x8 slice. The times are simulated.
256 devices in a mesh: fsdp: 32 (over z, y), tensor: 8 (over x, core).
Axes of the slice: x: 4, y: 4, z: 8, core: 2. Of those that a mesh axis runs over, the one named last changes fastest.
Arguments:
- context: bfloat16 [8192, 4096], P('fsdp', 'tensor'), may hold values from -6 to 6
- cotangent: bfloat16 [8192, 8192], P('fsdp', 'tensor'), may hold values from -0.0625 to 0.0625
- block_table: int32 [8, 64], P('tensor'), may hold values from 0 to 63, each once within a row
- left_stat: float32 [8, 64, 256, 256], P('tensor', 'fsdp'), may hold values from -1 to 5, as said below
- right_stat: float32 [8, 64, 256, 256], P('tensor', 'fsdp'), may hold values from -1 to 5, as said below
- root_left: float32 [8, 64, 256, 256], P('tensor', 'fsdp'), may hold values from -1 to 5, as said below
- root_right: float32 [8, 64, 256, 256], P('tensor', 'fsdp'), may hold values from -1 to 5, as said below
- second_moment: float32 [8, 64, 256, 256], P('tensor', 'fsdp'), may hold values from 0.3 to 3
Outputs:
- left_new: float32 [8, 64, 256, 256], P('tensor', 'fsdp')
- right_new: float32 [8, 64, 256, 256], P('tensor', 'fsdp')
- second_new: float32 [8, 64, 256, 256], P('tensor', 'fsdp')
- search_direction: bfloat16 [8, 512, 8192], P('tensor', 'fsdp')
Inputs may be any that keep to these rules, and one draw needn't show every extreme that they name: Each row of block_table names every block 0 to 63 once. `left_stat`: symmetric, with positive diagonal. `right_stat`: symmetric, with positive diagonal. `root_left`: symmetric, with positive diagonal. `root_right`: symmetric, with positive diagonal.
All inputs are finite; a program needn't handle non-finite values.
Results may differ from a plain program's by a relative error of at most 0.017.
Values may be sent and summed in bfloat16 or wider, within the bound.
A program may use at most 128 MiB of HBM per device.

v0:
```python
import jax
import jax.numpy as jnp
from jax import lax
from jax.sharding import Mesh
from jax.sharding import PartitionSpec as P

FSDP = ("fsdp_0", "fsdp_1")
decay_rate = 0.95


def own_rows(terms, axes):
    total = terms.astype(jnp.bfloat16)
    for axis in axes:
        total = lax.psum_scatter(total, axis, scatter_dimension=0, tiled=True)
    return total.astype(jnp.float32)


def per_device(
    context, cotangent, block_table, left_stat, right_stat, root_left, root_right, second_moment
):
    full_cot = lax.all_gather(cotangent, "tensor", axis=1, tiled=True)
    tokens_here, band_rows = context.shape
    model_width = full_cot.shape[1]
    block_size = left_stat.shape[-1]
    slot_count = left_stat.shape[1]
    groups = lax.axis_size(FSDP)
    position = lax.axis_index(FSDP)
    owner_table = block_table[0]
    col_bands = model_width // block_size
    strip_rows = band_rows // groups
    per_band = block_size // strip_rows
    my_blocks = lax.dynamic_slice_in_dim(owner_table, position * slot_count, slot_count)
    ctx_bands = context.reshape(tokens_here, band_rows // block_size, block_size)
    cot_bands = full_cot.reshape(tokens_here, col_bands, block_size)
    left_part = jnp.take(ctx_bands, owner_table // col_bands, axis=1)
    right_part = jnp.take(cot_bands, owner_table % col_bands, axis=1)
    blocks = jnp.einsum("tnb,tnc->nbc", left_part, right_part, preferred_element_type=jnp.float32)
    gradient = own_rows(
        blocks.reshape(slot_count * block_size * lax.axis_size(FSDP), block_size), FSDP
    )
    gradient = gradient.reshape(slot_count, block_size, block_size)
    highest = lax.Precision.HIGHEST
    gram_left = jnp.einsum("sij,skj->sik", gradient, gradient, precision=highest)
    gram_right = jnp.einsum("sji,sjk->sik", gradient, gradient, precision=highest)
    left_new = decay_rate * left_stat[0] + (1.0 - decay_rate) * gram_left / block_size
    right_new = decay_rate * right_stat[0] + (1.0 - decay_rate) * gram_right / block_size
    second_new = decay_rate * second_moment[0] + (1.0 - decay_rate) * gradient * gradient
    adam_step = gradient / (jnp.sqrt(second_new) + 1e-08)
    shaped = jnp.einsum("sij,sjk->sik", root_left[0], gradient, precision=highest)
    shaped = jnp.einsum("sij,sjk->sik", shaped, root_right[0], precision=highest)
    graft_ratio = jnp.sqrt(jnp.sum(adam_step * adam_step, axis=(1, 2))) / jnp.sqrt(
        jnp.sum(shaped * shaped, axis=(1, 2)) + 1e-06
    )
    direction = (shaped * graft_ratio[:, None, None]).astype(jnp.bfloat16)
    by_strip = direction.reshape(slot_count, per_band, strip_rows, block_size)
    targets = jnp.arange(groups, dtype=jnp.int32)
    chosen = jnp.take(by_strip, targets % per_band, axis=1)
    keep_mask = ((my_blocks // col_bands)[:, None] == (targets // per_band)[None, :]).astype(
        jnp.bfloat16
    )
    outgoing_rows = jnp.swapaxes(chosen * keep_mask[:, :, None, None], 0, 1)
    returned = lax.all_to_all(outgoing_rows, FSDP, split_axis=0, concat_axis=0, tiled=True)
    wanted = position // per_band * col_bands + jnp.arange(col_bands, dtype=jnp.int32)
    slot_ids = jnp.arange(owner_table.shape[0], dtype=jnp.int32)
    located = jnp.sum(
        jnp.where(owner_table[None, :] == wanted[:, None], slot_ids[None, :], 0), axis=1
    )
    flat_pieces = returned.reshape(groups * slot_count, strip_rows, block_size)
    pieces = jnp.take(flat_pieces, located, axis=0)
    result = jnp.swapaxes(pieces, 0, 1).reshape(strip_rows, model_width)
    return (left_new[None], right_new[None], second_new[None], result[None])


def solution(mesh):
    finer = Mesh(mesh.devices.reshape(8, 4, mesh.shape["tensor"]), ("fsdp_0", "fsdp_1", "tensor"))
    in_specs = (
        P(FSDP, "tensor"),
        P(FSDP, "tensor"),
        P("tensor", None),
        P("tensor", FSDP, None, None),
        P("tensor", FSDP, None, None),
        P("tensor", FSDP, None, None),
        P("tensor", FSDP, None, None),
        P("tensor", FSDP, None, None),
    )
    out_specs = (
        P("tensor", FSDP, None, None),
        P("tensor", FSDP, None, None),
        P("tensor", FSDP, None, None),
        P("tensor", FSDP, None),
    )
    return jax.shard_map(
        per_device, mesh=finer, in_specs=in_specs, out_specs=out_specs, check_vma=False
    )
```

profile of v0, /device:TPU:2, one launch (start us, length us, event | category | flops | bytes accessed | tf_op | source)
XLA Modules:
  0.0 236.2 jit_solution(10105942067028597240)
XLA Ops:
  7.2 2.1 copy.38
  9.4 1.1 copy.36
  10.5 0.1 copy.37
  10.6 0.7 fusion.28
  11.3 5.4 %gather_fusion = bf16[64,256,256]{2,1,0:T(8,128)(2,1)} fusion(bf16[256,2,256]{2,0,1:T(8,128)(2,1)S(1)} %copy.37, s32[1024]{0:T(1024)S(1)} %get-tuple-element.13), kind=kCustom, calls=%fused_computation | custom fusion | bytes 16777472 | tf_op jit(solution)/shard_map/jit(_take)/gather | solution.py:35
  16.7 30.3 %all-gather.2.cloned.1.call-done = bf16[256,8192]{0,1:T(8,128)(2,1)} async-done(((bf16[256,1024]{0,1:T(8,128)(2,1)}), bf16[256,8192]{0,1:T(8,128)(2,1)}) %all-gather.2.cloned.1.call-update) | async-done | bytes 4194320 | tf_op jit(solution)/shard_map/all_gather | solution.py:21
  47.0 6.4 %copy.39 = bf16[256,32,256]{2,0,1:T(8,128)(2,1)} copy(bf16[256,32,256]{0,2,1:T(8,128)(2,1)} %bitcast.93) | data formatting | bytes 8388608 | tf_op jit(solution)/shard_map/reshape | solution.py:34
  53.4 7.7 %gather_fusion.1 = bf16[64,256,256]{2,1,0:T(8,128)(2,1)} fusion(bf16[256,32,256]{2,0,1:T(8,128)(2,1)} %copy.39, s32[1024]{0:T(1024)S(1)} %get-tuple-element.12), kind=kCustom, calls=%fused_computation.1 | custom fusion | bytes 16777472 | tf_op jit(solution)/shard_map/jit(_take)/gather | solution.py:36
  61.1 11.4 %fusion.7 = bf16[64,256,256]{2,1,0:T(8,128)(2,1)} fusion(bf16[64,256,256]{2,1,0:T(8,128)(2,1)} %gather_fusion.1, pred[64]{0:T(512)(128)(4,1)S(1)} %get-tuple-element.7, bf16[64,256,256]{2,1,0:T(8,128)(2,1)} %gather_fusion, pred[64]{0:T(512)(128)(4,1)S(1)} %get-tuple-element.6), kind=kOutput, calls=%fused_computation.11 | convolution fusion | flops 2160066560 | bytes 25165952 | tf_op jit(solution)/shard_map/tnb,tnc->nbc/dot_general | solution.py:37
  72.6 96.0 %reduce-scatter.3.cloned.1.call-done = bf16[2048,256]{1,0:T(8,128)(2,1)} async-done(((bf16[16384,256]{1,0:T(8,128)(2,1)}), bf16[2048,256]{1,0:T(8,128)(2,1)}) %reduce-scatter.3.cloned.1.call-update) | async-done | bytes 1048592 | tf_op jit(solution)/shard_map/reduce_scatter | solution.py:14
  168.9 27.3 %reduce-scatter.5.cloned.1.call-done = bf16[512,256]{1,0:T(8,128)(2,1)} async-done(((bf16[2048,256]{1,0:T(8,128)(2,1)}), bf16[512,256]{1,0:T(8,128)(2,1)}) %reduce-scatter.5.cloned.1.call-update) | async-done | bytes 262160 | tf_op jit(solution)/shard_map/reduce_scatter | solution.py:14
  196.2 1.9 broadcast_multiply_fusion
  198.1 1.3 fusion.27
  199.5 1.3 fusion.25
  200.8 0.8 multiply_reduce_fusion
  201.8 0.6 gather_fusion.2
  202.4 1.0 select_multiply_fusion
  203.4 8.2 %all-to-all-start = ((bf16[32,2,16,256]{3,2,1,0:T(8,128)(2,1)}), bf16[32,2,16,256]{3,2,1,0:T(8,128)(2,1)S(1)}, u32[]{:S(2)}, u32[]{:S(2)}) async-start(bf16[32,2,16,256]{3,2,1,0:T(8,128)(2,1)} %select_multiply_fusion), calls=%async_computation.2 | async-start | bytes 1048576 | tf_op jit(solution)/shard_map/all_to_all | solution.py:62
  211.7 0.2 select_reduce_fusion
  211.9 1.1 fusion.14
  213.0 1.1 fusion.16
  214.0 14.0 %all-to-all-done = bf16[32,2,16,256]{3,2,1,0:T(8,128)(2,1)S(1)} async-done(((bf16[32,2,16,256]{3,2,1,0:T(8,128)(2,1)}), bf16[32,2,16,256]{3,2,1,0:T(8,128)(2,1)S(1)}, u32[]{:S(2)}, u32[]{:S(2)}) %all-to-all-start) | async-done | bytes 524320 | tf_op jit(solution)/shard_map/all_to_all | solution.py:62
  228.1 0.6 gather_fusion.3
  228.9 0.8 broadcast_in_dim_reshape.3
  (39 shorter events, 1.0 us)
Async XLA Ops:
  7.2 193.7 %copy-start = (f32[1,2,256,256]{3,2,1,0:T(8,128)S(1)}, f32[1,2,256,256]{3,2,1,0:T(8,128)}, u32[]{:S(2)}) copy-start(f32[1,2,256,256]{3,2,1,0:T(8,128)} %param.14) | copy-start | bytes 1572868
  7.2 39.8 %all-gather.2.cloned.1.call-start = ((), (), s32[]{:S(2)}) async-start(), calls=%async_computation.3 | async-start | bytes 4718592 | tf_op jit(solution)/shard_map/all_gather | solution.py:21
  9.3 159.3 %reduce-scatter.3.cloned.1.call-start = ((), (), s32[]{:S(2)}) async-start(), calls=%async_computation.4 | async-start | bytes 9437184 | tf_op jit(solution)/shard_map/reduce_scatter | solution.py:14
  11.3 5.4 %copy-start.6 = (s32[1,64]{1,0:T(1,128)S(1)}, s32[1,64]{1,0:T(1,128)}, u32[]{:S(2)}) copy-start(s32[1,64]{1,0:T(1,128)} %param.10) | copy-start | bytes 772
  72.5 123.7 %copy-start.2 = (f32[1,2,256,256]{3,2,1,0:T(8,128)S(1)}, f32[1,2,256,256]{3,2,1,0:T(8,128)}, u32[]{:S(2)}) copy-start(f32[1,2,256,256]{3,2,1,0:T(8,128)} %param.15) | copy-start | bytes 1572868
  72.5 127.0 %copy-start.5 = (f32[1,2,256,256]{3,2,1,0:T(8,128)S(1)}, f32[1,2,256,256]{3,2,1,0:T(8,128)}, u32[]{:S(2)}) copy-start(f32[1,2,256,256]{3,2,1,0:T(8,128)} %param.13) | copy-start | bytes 1572868
  72.5 139.4 %copy-start.3 = (f32[1,2,256,256]{3,2,1,0:T(8,128)S(1)}, f32[1,2,256,256]{3,2,1,0:T(8,128)}, u32[]{:S(2)}) copy-start(f32[1,2,256,256]{3,2,1,0:T(8,128)} %param.12) | copy-start | bytes 1572868
  72.5 140.5 %copy-start.4 = (f32[1,2,256,256]{3,2,1,0:T(8,128)S(1)}, f32[1,2,256,256]{3,2,1,0:T(8,128)}, u32[]{:S(2)}) copy-start(f32[1,2,256,256]{3,2,1,0:T(8,128)} %param.11) | copy-start | bytes 1572868
  72.5 123.7 %reduce-scatter.5.cloned.1.call-start = ((), (), s32[]{:S(2)}) async-start(), calls=%async_computation.5 | async-start | bytes 1310720 | tf_op jit(solution)/shard_map/reduce_scatter | solution.py:14
  196.2 15.7 %copy-start.1 = (bf16[512,256]{1,0:T(8,128)(2,1)S(1)}, bf16[512,256]{1,0:T(8,128)(2,1)}, u32[]{:S(2)}) copy-start(bf16[512,256]{1,0:T(8,128)(2,1)} %reduce-scatter.5.cloned.1.call-done) | copy-start | bytes 786436
  203.4 24.7 %all-to-all-start = ((bf16[32,2,16,256]{3,2,1,0:T(8,128)(2,1)}), bf16[32,2,16,256]{3,2,1,0:T(8,128)(2,1)S(1)}, u32[]{:S(2)}, u32[]{:S(2)}) async-start(bf16[32,2,16,256]{3,2,1,0:T(8,128)(2,1)} %select_multiply_fusion), calls=%async_computation.2 | async-start | bytes 1048576 | tf_op jit(solution)/shard_map/all_to_all | solution.py:62
Sparse Core Ops, SparseCore 0:
  10.4 36.5 all-gather.1
  72.7 95.8 reduce-scatter.2
  171.1 25.0 reduce-scatter.4
where the time goes:
time: 237 us; the launch traced here: 236 us
  waiting for transfers between devices  168 us (71%)
  local copies, waits for them, and re-layouts  25 us (11%)
  matrix products  15.6 us (7%)
  between operations  13.9 us (6%)
  starting transfers between devices  8.37 us (4%)
  other arithmetic  5.64 us (2%)
    reduce_scatter x2, waiting for transfers between devices, own_rows(): total = lax.psum_scatter(total, axis, scatter_dimension=0, tiled=True)  123 us
    all_gather x1, waiting for transfers between devices, per_device(): full_cot = lax.all_gather(cotangent, 'tensor', axis=1, tiled=True)  30.3 us
    all_to_all x1, waiting for transfers between devices, per_device(): lax.all_to_all(outgoing_rows, FSDP, split_axis=0, concat_axis=0, tiled=True)  14 us
    dot_general x1, matrix products, per_device(): jnp.einsum('tnb,tnc->nbc', left_part, right_part, preferred_element_type=...  11.4 us
    all_to_all x1, starting transfers between devices, per_device(): lax.all_to_all(outgoing_rows, FSDP, split_axis=0, concat_axis=0, tiled=True)  8.25 us
    gather x1, local copies, waits for them, and re-layouts, per_device(): right_part = jnp.take(cot_bands, owner_table % col_bands, axis=1)  7.71 us
    reshape x1, local copies, waits for them, and re-layouts, per_device(): cot_bands = full_cot.reshape(tokens_here, col_bands, block_size)  6.43 us
    gather x1, local copies, waits for them, and re-layouts, per_device(): left_part = jnp.take(ctx_bands, owner_table // col_bands, axis=1)  5.37 us
  transfers between devices with their start and end apart: 4, of which 4 were waited for; matrix products, arithmetic and copies ran while one was open for 4% of the time, Pallas kernels for 0%

commit v1 on v0

--- a/solution.py
+++ b/solution.py
@@ -18,7 +18,24 @@
 def per_device(
     context, cotangent, block_table, left_stat, right_stat, root_left, root_right, second_moment
 ):
-    full_cot = lax.all_gather(cotangent, "tensor", axis=1, tiled=True)
+    size, position_2, rows = (lax.axis_size("tensor"), lax.axis_index("tensor"), cotangent.shape[1])
+    right = [(i, (i + 1) % size) for i in range(size)]
+    backward = [(i, (i - 1) % size) for i in range(size)]
+    out = jnp.zeros((*cotangent.shape[:1], size * rows, *cotangent.shape[1 + 1 :]), cotangent.dtype)
+    out = lax.dynamic_update_slice_in_dim(out, cotangent, position_2 * rows, axis=1)
+    from_left = from_right = cotangent
+    middle = size // 2
+    for lap in range(1, middle + 1):
+        from_left = lax.ppermute(from_left, "tensor", right)
+        out = lax.dynamic_update_slice_in_dim(
+            out, from_left, (position_2 - lap) % size * rows, axis=1
+        )
+        if lap < size - middle:
+            from_right = lax.ppermute(from_right, "tensor", backward)
+            out = lax.dynamic_update_slice_in_dim(
+                out, from_right, (position_2 + lap) % size * rows, axis=1
+            )
+    full_cot = out
     tokens_here, band_rows = context.shape
     model_width = full_cot.shape[1]
     block_size = left_stat.shape[-1]

time: 237 us -> 242 us (1.021)
  waiting for transfers between devices: 168 us -> 158 us
  local copies, waits for them, and re-layouts: 25 us -> 34.2 us
  starting transfers between devices: 8.37 us -> 13.9 us
    all_gather x1 -> x0, waiting for transfers between devices: 30.3 us -> none  [per_device(): full_cot = lax.all_gather(cotangent, 'tensor', axis=1, tiled=True)]
    ppermute x0 -> x7, waiting for transfers between devices: none -> 17.8 us  [the longest x4 16.4 us: per_device(): from_left = lax.ppermute(from_left, 'tensor', right)]
    dynamic_update_slice x0 -> x8, local copies, waits for them, and re-layouts: none -> 7.75 us  [the longest x4 4.43 us: per_device(): lax.dynamic_update_slice_in_dim(out, from_left, (position_2 - lap) % size...]
    ppermute x0 -> x7, starting transfers between devices: none -> 5.45 us  [the longest x3 5.43 us: per_device(): from_right = lax.ppermute(from_right, 'tensor', backward)]
    reduce_scatter x2, waiting for transfers between devices: 123 us -> 126 us  [own_rows(): total = lax.psum_scatter(total, axis, scatter_dimension=0, tiled=True)]
  transfers between devices with their start and end apart: 4 -> 10, of which waited for: 4 -> 7; matrix products, arithmetic and copies ran while one was open for 4% -> 8% of each run, Pallas kernels for 0% -> 0%
where the time goes in v1:
time: 242 us
  waiting for transfers between devices  158 us (65%)
  local copies, waits for them, and re-layouts  34.2 us (14%)
  matrix products  15.6 us (6%)
  between operations  14.4 us (6%)
  starting transfers between devices  13.9 us (6%)
  other arithmetic  5.63 us (2%)
    reduce_scatter x2, waiting for transfers between devices, own_rows(): total = lax.psum_scatter(total, axis, scatter_dimension=0, tiled=True)  126 us
    ppermute x4, waiting for transfers between devices, per_device(): from_left = lax.ppermute(from_left, 'tensor', right)  16.4 us
    all_to_all x1, waiting for transfers between devices, per_device(): lax.all_to_all(outgoing_rows, FSDP, split_axis=0, concat_axis=0, tiled=True)  14 us
    dot_general x1, matrix products, per_device(): jnp.einsum('tnb,tnc->nbc', left_part, right_part, preferred_element_type=...  11.4 us
    all_to_all x1, starting transfers between devices, per_device(): lax.all_to_all(outgoing_rows, FSDP, split_axis=0, concat_axis=0, tiled=True)  8.34 us
    gather x1, local copies, waits for them, and re-layouts, per_device(): right_part = jnp.take(cot_bands, owner_table % col_bands, axis=1)  7.74 us
    reshape x1, local copies, waits for them, and re-layouts, per_device(): cot_bands = full_cot.reshape(tokens_here, col_bands, block_size)  6.44 us
    ppermute x3, starting transfers between devices, per_device(): from_right = lax.ppermute(from_right, 'tensor', backward)  5.43 us
  transfers between devices with their start and end apart: 10, of which 7 were waited for; matrix products, arithmetic and copies ran while one was open for 8% of the time, Pallas kernels for 0%

profile of v1, /device:TPU:2, one launch (start us, length us, event | category | flops | bytes accessed | tf_op | source)
XLA Modules:
  0.0 241.7 jit_solution(16408934852915558418)
XLA Ops:
  7.2 1.3 copy.42
  8.5 1.7 collective-permute-start.1
  10.3 6.9 %collective-permute-done = bf16[256,1024]{0,1:T(8,128)(2,1)S(1)} collective-permute-done((bf16[256,1024]{0,1:T(8,128)(2,1)S(1)}, bf16[256,1024]{0,1:T(8,128)(2,1)S(1)}, u32[]{:S(2)}, u32[]{:S(2)}) %collective-permute-start) | collective-permute-done | bytes 524320 | tf_op jit(solution)/shard_map/ppermute | solution.py:29
  17.2 2.0 collective-permute-start.3
  19.8 5.9 %collective-permute-done.2 = bf16[256,1024]{0,1:T(8,128)(2,1)S(1)} collective-permute-done((bf16[256,1024]{0,1:T(8,128)(2,1)S(1)}, bf16[256,1024]{0,1:T(8,128)(2,1)S(1)}, u32[]{:S(2)}, u32[]{:S(2)}) %collective-permute-start.2) | collective-permute-done | bytes 524320 | tf_op jit(solution)/shard_map/ppermute | solution.py:29
  25.9 1.1 copy.40
  27.2 5.4 %gather_fusion = bf16[64,256,256]{2,1,0:T(8,128)(2,1)} fusion(bf16[256,2,256]{2,0,1:T(8,128)(2,1)S(1)} %copy.41, s32[1024]{0:T(1024)S(1)} %get-tuple-element.13), kind=kCustom, calls=%fused_computation | custom fusion | bytes 16777472 | tf_op jit(solution)/shard_map/jit(_take)/gather | solution.py:52
  32.5 2.2 broadcast_in_dim.69
  35.6 1.7 collective-permute-start.5
  40.7 1.9 constant_dynamic-update-slice_fusion.2
  42.6 1.4 collective-permute-done.5
  44.8 3.6 %collective-permute-done.6 = bf16[256,1024]{0,1:T(8,128)(2,1)S(1)} collective-permute-done((bf16[256,1024]{0,1:T(8,128)(2,1)}, bf16[256,1024]{0,1:T(8,128)(2,1)S(1)}, u32[]{:S(2)}, u32[]{:S(2)}) %collective-permute-start.6) | collective-permute-done | bytes 524320 | tf_op jit(solution)/shard_map/ppermute | solution.py:29
  49.2 6.4 %copy.45 = bf16[256,32,256]{2,0,1:T(8,128)(2,1)} copy(bf16[256,32,256]{0,2,1:T(8,128)(2,1)} %bitcast.6) | data formatting | bytes 8388608 | tf_op jit(solution)/shard_map/reshape | solution.py:51
  55.7 7.7 %gather_fusion.1 = bf16[64,256,256]{2,1,0:T(8,128)(2,1)} fusion(bf16[256,32,256]{2,0,1:T(8,128)(2,1)} %copy.45, s32[1024]{0:T(1024)S(1)} %get-tuple-element.12), kind=kCustom, calls=%fused_computation.1 | custom fusion | bytes 16777472 | tf_op jit(solution)/shard_map/jit(_take)/gather | solution.py:53
  63.4 11.4 %fusion.7 = bf16[64,256,256]{2,1,0:T(8,128)(2,1)} fusion(bf16[64,256,256]{2,1,0:T(8,128)(2,1)} %gather_fusion.1, pred[64]{0:T(512)(128)(4,1)S(1)} %get-tuple-element.7, bf16[64,256,256]{2,1,0:T(8,128)(2,1)} %gather_fusion, pred[64]{0:T(512)(128)(4,1)S(1)} %get-tuple-element.6), kind=kOutput, calls=%fused_computation.11 | convolution fusion | flops 2160066560 | bytes 25165952 | tf_op jit(solution)/shard_map/tnb,tnc->nbc/dot_general | solution.py:54
  74.8 98.9 %reduce-scatter.3.cloned.1.call-done = bf16[2048,256]{1,0:T(8,128)(2,1)} async-done(((bf16[16384,256]{1,0:T(8,128)(2,1)}), bf16[2048,256]{1,0:T(8,128)(2,1)}) %reduce-scatter.3.cloned.1.call-update) | async-done | bytes 1048592 | tf_op jit(solution)/shard_map/reduce_scatter | solution.py:14
  174.0 27.2 %reduce-scatter.5.cloned.1.call-done = bf16[512,256]{1,0:T(8,128)(2,1)} async-done(((bf16[2048,256]{1,0:T(8,128)(2,1)}), bf16[512,256]{1,0:T(8,128)(2,1)}) %reduce-scatter.5.cloned.1.call-update) | async-done | bytes 262160 | tf_op jit(solution)/shard_map/reduce_scatter | solution.py:14
  201.3 1.8 broadcast_multiply_fusion
  203.1 1.4 fusion.27
  204.7 1.4 fusion.25
  208.5 8.3 %all-to-all-start = ((bf16[32,2,16,256]{3,2,1,0:T(8,128)(2,1)}), bf16[32,2,16,256]{3,2,1,0:T(8,128)(2,1)S(1)}, u32[]{:S(2)}, u32[]{:S(2)}) async-start(bf16[32,2,16,256]{3,2,1,0:T(8,128)(2,1)} %select_multiply_fusion), calls=%async_computation.2 | async-start | bytes 1048576 | tf_op jit(solution)/shard_map/all_to_all | solution.py:79
  217.1 1.1 fusion.14
  218.2 1.1 fusion.16
  219.3 14.0 %all-to-all-done = bf16[32,2,16,256]{3,2,1,0:T(8,128)(2,1)S(1)} async-done(((bf16[32,2,16,256]{3,2,1,0:T(8,128)(2,1)}), bf16[32,2,16,256]{3,2,1,0:T(8,128)(2,1)S(1)}, u32[]{:S(2)}, u32[]{:S(2)}) %all-to-all-start) | async-done | bytes 524320 | tf_op jit(solution)/shard_map/all_to_all | solution.py:79
  (63 shorter events, 11.5 us)
Async XLA Ops:
  7.2 198.9 %copy-start = (f32[1,2,256,256]{3,2,1,0:T(8,128)S(1)}, f32[1,2,256,256]{3,2,1,0:T(8,128)}, u32[]{:S(2)}) copy-start(f32[1,2,256,256]{3,2,1,0:T(8,128)} %param.14) | copy-start | bytes 1572868
  7.2 166.5 %reduce-scatter.3.cloned.1.call-start = ((), (), s32[]{:S(2)}) async-start(), calls=%async_computation.3 | async-start | bytes 9437184 | tf_op jit(solution)/shard_map/reduce_scatter | solution.py:14
  8.5 8.6 %collective-permute-start = (bf16[256,1024]{0,1:T(8,128)(2,1)S(1)}, bf16[256,1024]{0,1:T(8,128)(2,1)S(1)}, u32[]{:S(2)}, u32[]{:S(2)}) collective-permute-start(bf16[256,1024]{0,1:T(8,128)(2,1)S(1)} %copy.42), channel_id=1, source_target_pairs={{0,1},{1,2},{2,3},{3,4},{4,5},{5,6},{6,7},{7,0},{8,9},{9,10},{10,1... | collective-permute-start | bytes 1572872 | tf_op jit(solution)/shard_map/ppermute | solution.py:29
  8.5 8.6 %collective-permute-start.1 = (bf16[256,1024]{0,1:T(8,128)(2,1)S(1)}, bf16[256,1024]{0,1:T(8,128)(2,1)S(1)}, u32[]{:S(2)}, u32[]{:S(2)}) collective-permute-start(bf16[256,1024]{0,1:T(8,128)(2,1)S(1)} %copy.42), channel_id=1, source_target_pairs={{0,7},{1,0},{2,1},{3,2},{4,3},{5,4},{6,5},{7,6},{8,15},{9,8},{10,9... | collective-permute-start | bytes 1572872 | tf_op jit(solution)/shard_map/ppermute | solution.py:34
  17.1 8.6 %copy-start.6 = (bf16[256,1024]{0,1:T(8,128)(2,1)}, bf16[256,1024]{0,1:T(8,128)(2,1)S(1)}, u32[]{:S(2)}) copy-start(bf16[256,1024]{0,1:T(8,128)(2,1)S(1)} %collective-permute-done) | copy-start | bytes 1572868
  17.1 8.6 %collective-permute-start.2 = (bf16[256,1024]{0,1:T(8,128)(2,1)S(1)}, bf16[256,1024]{0,1:T(8,128)(2,1)S(1)}, u32[]{:S(2)}, u32[]{:S(2)}) collective-permute-start(bf16[256,1024]{0,1:T(8,128)(2,1)S(1)} %collective-permute-done), channel_id=1, source_target_pairs={{0,1},{1,2},{2,3},{3,4},{4,5},{5,6},{6,7},{7,0},{8,9},{9,10},{10,1... | collective-permute-start | bytes 1572872 | tf_op jit(solution)/shard_map/ppermute | solution.py:29
  17.2 18.5 %collective-permute-start.3 = (bf16[256,1024]{0,1:T(8,128)(2,1)S(1)}, bf16[256,1024]{0,1:T(8,128)(2,1)S(1)}, u32[]{:S(2)}, u32[]{:S(2)}) collective-permute-start(bf16[256,1024]{0,1:T(8,128)(2,1)S(1)} %collective-permute-done.1), channel_id=1, source_target_pairs={{0,7},{1,0},{2,1},{3,2},{4,3},{5,4},{6,5},{7,6},{8,15},{9,8},{10,9... | collective-permute-start | bytes 1572872 | tf_op jit(solution)/shard_map/ppermute | solution.py:34
  25.8 12.4 %collective-permute-start.4 = (bf16[256,1024]{0,1:T(8,128)(2,1)S(1)}, bf16[256,1024]{0,1:T(8,128)(2,1)}, u32[]{:S(2)}, u32[]{:S(2)}) collective-permute-start(bf16[256,1024]{0,1:T(8,128)(2,1)S(1)} %collective-permute-done.2), channel_id=1, source_target_pairs={{0,1},{1,2},{2,3},{3,4},{4,5},{5,6},{6,7},{7,0},{8,9},{9,10},{10,1... | collective-permute-start | bytes 1572872 | tf_op jit(solution)/shard_map/ppermute | solution.py:29
  32.5 3.1 %copy-start.8 = (s32[1,64]{1,0:T(1,128)S(1)}, s32[1,64]{1,0:T(1,128)}, u32[]{:S(2)}) copy-start(s32[1,64]{1,0:T(1,128)} %param.10) | copy-start | bytes 772
  32.5 4.8 %copy-start.7 = (bf16[256,1024]{0,1:T(8,128)(2,1)S(1)}, bf16[256,1024]{0,1:T(8,128)(2,1)}, u32[]{:S(2)}) copy-start(bf16[256,1024]{0,1:T(8,128)(2,1)} %copy-done.6) | copy-start | bytes 1572868
  35.6 8.4 %collective-permute-start.5 = (bf16[256,1024]{0,1:T(8,128)(2,1)S(1)}, bf16[256,1024]{0,1:T(8,128)(2,1)S(1)}, u32[]{:S(2)}, u32[]{:S(2)}) collective-permute-start(bf16[256,1024]{0,1:T(8,128)(2,1)S(1)} %collective-permute-done.3), channel_id=1, source_target_pairs={{0,7},{1,0},{2,1},{3,2},{4,3},{5,4},{6,5},{7,6},{8,15},{9,8},{10,9... | collective-permute-start | bytes 1572872 | tf_op jit(solution)/shard_map/ppermute | solution.py:34
  38.2 10.2 %collective-permute-start.6 = (bf16[256,1024]{0,1:T(8,128)(2,1)}, bf16[256,1024]{0,1:T(8,128)(2,1)S(1)}, u32[]{:S(2)}, u32[]{:S(2)}) collective-permute-start(bf16[256,1024]{0,1:T(8,128)(2,1)} %collective-permute-done.4), channel_id=1, source_target_pairs={{0,1},{1,2},{2,3},{3,4},{4,5},{5,6},{6,7},{7,0},{8,9},{9,10},{10,1... | collective-permute-start | bytes 1572872 | tf_op jit(solution)/shard_map/ppermute | solution.py:29
  74.8 126.5 %copy-start.2 = (f32[1,2,256,256]{3,2,1,0:T(8,128)S(1)}, f32[1,2,256,256]{3,2,1,0:T(8,128)}, u32[]{:S(2)}) copy-start(f32[1,2,256,256]{3,2,1,0:T(8,128)} %param.15) | copy-start | bytes 1572868
  74.8 129.9 %copy-start.5 = (f32[1,2,256,256]{3,2,1,0:T(8,128)S(1)}, f32[1,2,256,256]{3,2,1,0:T(8,128)}, u32[]{:S(2)}) copy-start(f32[1,2,256,256]{3,2,1,0:T(8,128)} %param.13) | copy-start | bytes 1572868
  74.8 126.5 %reduce-scatter.5.cloned.1.call-start = ((), (), s32[]{:S(2)}) async-start(), calls=%async_computation.4 | async-start | bytes 1310720 | tf_op jit(solution)/shard_map/reduce_scatter | solution.py:14
  203.1 14.0 %copy-start.1 = (bf16[512,256]{1,0:T(8,128)(2,1)S(1)}, bf16[512,256]{1,0:T(8,128)(2,1)}, u32[]{:S(2)}) copy-start(bf16[512,256]{1,0:T(8,128)(2,1)} %reduce-scatter.5.cloned.1.call-done) | copy-start | bytes 786436
  203.1 14.0 %copy-start.3 = (f32[1,2,256,256]{3,2,1,0:T(8,128)S(1)}, f32[1,2,256,256]{3,2,1,0:T(8,128)}, u32[]{:S(2)}) copy-start(f32[1,2,256,256]{3,2,1,0:T(8,128)} %param.12) | copy-start | bytes 1572868
  204.7 13.5 %copy-start.4 = (f32[1,2,256,256]{3,2,1,0:T(8,128)S(1)}, f32[1,2,256,256]{3,2,1,0:T(8,128)}, u32[]{:S(2)}) copy-start(f32[1,2,256,256]{3,2,1,0:T(8,128)} %param.11) | copy-start | bytes 1572868
  208.5 24.8 %all-to-all-start = ((bf16[32,2,16,256]{3,2,1,0:T(8,128)(2,1)}), bf16[32,2,16,256]{3,2,1,0:T(8,128)(2,1)S(1)}, u32[]{:S(2)}, u32[]{:S(2)}) async-start(bf16[32,2,16,256]{3,2,1,0:T(8,128)(2,1)} %select_multiply_fusion), calls=%async_computation.2 | async-start | bytes 1048576 | tf_op jit(solution)/shard_map/all_to_all | solution.py:79
Sparse Core Ops, SparseCore 0:
  74.9 98.7 reduce-scatter.2
  176.3 24.9 reduce-scatter.4
